TPU v7x, 512 devices: a whole 4x8x8 slice. The times are simulated.
512 devices in a mesh: ctx: 64 (over y, z_hi, core), fsdp: 8 (over z_lo, x).
Axes of the slice: x: 4, y: 8, z: 8 (z_hi: 4, z_lo: 2; z = z_hi * 2 + z_lo), core: 2. Of those that a mesh axis runs over, the one named last changes fastest.
Arguments:
- query_act: bfloat16 [16384, 3072], P('ctx', 'fsdp'), may hold values from -10 to 10
- key_act: bfloat16 [16384, 3072], P('ctx', 'fsdp'), may hold values from -4 to 4
- value_act: bfloat16 [16384, 3072], P('ctx', 'fsdp'), may hold values from -6 to 6
- resid_in: bfloat16 [16384, 3072], P('ctx', 'fsdp'), may hold values from -60 to 60
- gate_vec: float32 [3072], P('fsdp'), may hold values from 0.5 to 2.5
- mod_scale: float32 [3072], P('fsdp'), may hold values from -2.5 to 2.5
- mod_shift: float32 [3072], P('fsdp'), may hold values from -3 to 3
- w_up: bfloat16 [3072, 6912], P(('ctx', 'fsdp')), may hold values from -0.109375 to 0.109375
- bias_up: float32 [6912], P('fsdp'), may hold values from -3 to 3
Outputs:
- residual: bfloat16 [16384, 3072], P('ctx', 'fsdp')
- hidden: bfloat16 [16384, 6912], P('ctx', 'fsdp')
All inputs are finite; a program needn't handle non-finite values.
Results may differ from a plain program's by a relative error of at most 0.0059.
Values may be sent and summed in bfloat16 or wider, within the bound.
A program may use at most 64 MiB of HBM per device.

v0:
```python
import math

import jax
import jax.numpy as jnp
from jax import lax
from jax.sharding import PartitionSpec as P

HEAD = 128
D = 3072


def padded_2(cells, sides, width):
    for axis, dim in sides:
        count = lax.axis_size(axis)
        ends = count - 1
        head = lax.slice_in_dim(cells, 0, width, axis=dim)
        tail = lax.slice_in_dim(cells, cells.shape[dim] - width, cells.shape[dim], axis=dim)
        cells = jnp.concatenate(
            [
                lax.ppermute(tail, axis, [(i, (i + 1) % count) for i in range(ends)]),
                cells,
                lax.ppermute(head, axis, [((i + 1) % count, i) for i in range(ends)]),
            ],
            axis=dim,
        )
    return cells


def shards(query_act, key_act, value_act, resid_in, gate_vec, mod_scale, mod_shift, w_up, bias_up):
    tok_rows = query_act.shape[0]
    feat_width = query_act.shape[1]
    reach_rows = tok_rows // 2
    ctx_count = lax.axis_size("ctx")
    seq_total = tok_rows * ctx_count
    stacked = jnp.stack([key_act, value_act])
    padded = padded_2(stacked, (("ctx", 1),), reach_rows)
    first_pos = lax.axis_index("ctx") * tok_rows
    query_pos = first_pos + jnp.arange(tok_rows, dtype=jnp.int32)
    key_pos = first_pos - reach_rows + jnp.arange(tok_rows + 2 * reach_rows, dtype=jnp.int32)
    allowed = (
        (jnp.abs(query_pos[:, None] - key_pos[None, :]) <= reach_rows)
        & (key_pos[None, :] >= 0)
        & (key_pos[None, :] < seq_total)
    )
    scale_qk = 1.0 / math.sqrt(HEAD)
    head_outputs = []
    for head_idx in range(feat_width // HEAD):
        head_cols = slice(head_idx * HEAD, (head_idx + 1) * HEAD)
        scores = (
            jnp.einsum(
                "qd,kd->qk",
                query_act[:, head_cols],
                padded[0, :, head_cols],
                preferred_element_type=jnp.float32,
            )
            * scale_qk
        )
        masked = jnp.where(allowed, scores, -jnp.inf)
        row_max = jnp.max(masked, axis=1, keepdims=True)
        exp_terms = jnp.exp(masked - row_max)
        attn_probs = (exp_terms / jnp.sum(exp_terms, axis=1, keepdims=True)).astype(jnp.bfloat16)
        head_outputs.append(
            jnp.dot(attn_probs, padded[1, :, head_cols], preferred_element_type=jnp.float32)
        )
    attended = jnp.concatenate(head_outputs, axis=1).astype(jnp.bfloat16)
    residual_out = (resid_in.astype(jnp.float32) + gate_vec * attended.astype(jnp.float32)).astype(
        jnp.bfloat16
    )
    rows_float = residual_out.astype(jnp.float32)
    row_sum = lax.psum(jnp.sum(rows_float, axis=1), "fsdp")
    mean_val = row_sum / D
    centered = rows_float - mean_val[:, None]
    var_val = lax.psum(jnp.sum(centered * centered, axis=1), "fsdp") / D
    normed = (
        centered * lax.rsqrt(var_val + 1e-06)[:, None] * (1.0 + mod_scale) + mod_shift
    ).astype(jnp.bfloat16)
    full_feat = lax.all_gather(normed, "fsdp", axis=1, tiled=True)
    strided = lax.all_gather(w_up, "ctx", axis=0, tiled=True)
    regrouped = lax.all_to_all(strided, "fsdp", split_axis=1, concat_axis=0, tiled=True)
    fsdp_count = lax.axis_size("fsdp")
    row_width = w_up.shape[0]
    permuted = (
        full_feat.reshape(tok_rows, ctx_count, fsdp_count, row_width)
        .transpose(0, 2, 1, 3)
        .reshape(tok_rows, -1)
    )
    pre_act = jnp.dot(permuted, regrouped, preferred_element_type=jnp.float32)
    hidden = jax.nn.gelu(pre_act + bias_up, approximate=True).astype(jnp.bfloat16)
    return (residual_out, hidden)


def solution(mesh):
    placed = (
        P("ctx", "fsdp"),
        P("ctx", "fsdp"),
        P("ctx", "fsdp"),
        P("ctx", "fsdp"),
        P("fsdp"),
        P("fsdp"),
        P("fsdp"),
        P(("ctx", "fsdp"), None),
        P("fsdp"),
    )
    return jax.shard_map(
        shards,
        mesh=mesh,
        in_specs=placed,
        out_specs=(P("ctx", "fsdp"), P("ctx", "fsdp")),
        check_vma=False,
    )
```

profile of v0, /device:TPU:1, one launch (start us, length us, event | category | flops | bytes accessed | tf_op | source)
XLA Modules:
  0.0 303.3 jit_solution(431408384966726718)
XLA Ops:
  8.0 0.0 all-gather.6.cloned.1.call-start
  8.0 0.7 all-gather.6.cloned.1.call-update
  8.7 109.5 %all-gather.6.cloned.1.call-done = bf16[64,6,6912]{2,1,0:T(8,128)(2,1)} async-done(((bf16[1,6,6912]{2,1,0:T(8,128)(2,1)}), bf16[64,6,6912]{2,1,0:T(8,128)(2,1)}) %all-gather.6.cloned.1.call-update) | async-done | bytes 5308432 | tf_op jit(solution)/shard_map/all_gather | solution.py:78
  118.2 13.9 %all_to_all.14 = bf16[384,8,864]{2,1,0:T(8,128)(2,1)} reshape(bf16[64,6,6912]{2,1,0:T(8,128)(2,1)} %all-gather.6.cloned.1.call-done) | data formatting | bytes 10616832 | tf_op jit(solution)/shard_map/all_to_all | solution.py:79
  132.2 8.4 %copy.19 = bf16[384,8,864]{0,2,1:T(8,128)(2,1)} copy(bf16[384,8,864]{2,1,0:T(8,128)(2,1)} %all_to_all.14) | data formatting | bytes 10616832 | tf_op jit(solution)/shard_map/all_to_all | solution.py:79
  140.6 4.8 %all-to-all-start = ((bf16[384,8,864]{0,2,1:T(8,128)(2,1)}), bf16[384,8,864]{0,2,1:T(8,128)(2,1)}, u32[]{:S(2)}, u32[]{:S(2)}) async-start(bf16[384,8,864]{0,2,1:T(8,128)(2,1)} %copy.19), calls=%async_computation | async-start | bytes 10616832 | tf_op jit(solution)/shard_map/all_to_all | solution.py:79
  145.5 0.0 copy-start.6
  145.5 0.0 all-gather.4.cloned.1.call-start
  145.5 0.0 copy-done
  145.6 0.0 copy-done.1
  145.6 2.1 collective-permute-start
  147.8 2.2 collective-permute-start.1
  150.0 0.0 copy-done.2
  150.0 0.1 copy.17
  150.2 0.0 copy-done.5
  150.2 55.0 %collective-permute-done = bf16[2,128,384]{2,1,0:T(8,128)(2,1)S(1)} collective-permute-done((bf16[2,128,384]{2,1,0:T(8,128)(2,1)S(1)}, bf16[2,128,384]{2,1,0:T(8,128)(2,1)S(1)}, u32[]{:S(2)}, u32[]{:S(2)}) %collective-permute-start) | collective-permute-done | bytes 196640 | tf_op jit(solution)/shard_map/ppermute | solution.py:20
  205.2 0.0 collective-permute-done.1
  205.2 0.1 pad_maximum_fusion
  205.3 0.0 copy-done.6
  205.3 0.3 fusion.31
  205.7 0.1 fusion.20
  205.8 0.3 fusion.32
  206.1 0.1 fusion.19
  206.3 0.3 fusion.33
  206.6 0.1 fusion.18
  206.7 0.3 convolution_convert_fusion
  207.0 0.3 convolution_convert_fusion.1
  207.3 0.0 copy-start.3
  207.3 0.0 copy-start.4
  207.3 0.3 convolution_convert_fusion.2
  207.6 0.4 copy-done.3
  207.9 0.2 convert_reduce_fusion
  208.1 19.0 %psum.14 = f32[256]{0:T(256)S(1)} all-reduce(f32[256]{0:T(256)S(1)} %get-tuple-element.8), channel_id=1, replica_groups=mesh['ctx'=64,'fsdp'=8] {'fsdp'}, use_global_device_ids=true, to_apply=%region_7.8 | all-reduce | flops 256 | bytes 2048 | tf_op jit(solution)/shard_map/psum | solution.py:70
  227.1 0.1 fusion.21
  227.2 12.6 %psum.15 = f32[256]{0:T(256)S(1)} all-reduce(f32[256]{0:T(256)S(1)} %fusion.21), channel_id=1, replica_groups=mesh['ctx'=64,'fsdp'=8] {'fsdp'}, use_global_device_ids=true, to_apply=%region_9.10 | all-reduce | flops 256 | bytes 2048 | tf_op jit(solution)/shard_map/psum | solution.py:73
  239.8 0.0 copy-done.4
  239.8 0.9 fusion.24
  240.7 0.0 all-gather.4.cloned.1.call-update
  240.7 0.8 copy.21
  241.5 41.8 %all-gather.4.cloned.1.call-done = bf16[256,3072]{0,1:T(8,128)(2,1)} async-done(((bf16[256,384]{0,1:T(8,128)(2,1)}), bf16[256,3072]{0,1:T(8,128)(2,1)}) %all-gather.4.cloned.1.call-update) | async-done | bytes 1572880 | tf_op jit(solution)/shard_map/all_gather | solution.py:77
  283.3 2.5 reshape.41
  285.8 1.5 copy.18
  287.2 2.6 reshape.42
  289.8 0.0 all-to-all-done
  289.8 0.0 copy-start.7
  289.8 3.5 %copy.22 = bf16[8,108,8,384]{3,2,0,1:T(8,128)(2,1)S(1)} copy(bf16[8,108,8,384]{3,2,1,0:T(8,128)(2,1)} %bitcast.14) | data formatting | bytes 10616832 | tf_op jit(solution)/shard_map/all_to_all | solution.py:79
  293.4 0.0 copy-done.7
  293.4 2.5 fusion.13
  (11 shorter events, 0.1 us)
Async XLA Ops:
  8.0 110.2 %all-gather.6.cloned.1.call-start = ((), (), s32[]{:S(2)}) async-start(), calls=%async_computation.2 | async-start | bytes 7188480 | tf_op jit(solution)/shard_map/all_gather | solution.py:78
  140.6 4.9 %copy-start = (bf16[256,384]{1,0:T(8,128)(2,1)S(1)}, bf16[256,384]{1,0:T(8,128)(2,1)}, u32[]{:S(2)}) copy-start(bf16[256,384]{1,0:T(8,128)(2,1)} %param.10) | copy-start | bytes 589828
  140.6 4.9 %copy-start.1 = (bf16[256,384]{1,0:T(8,128)(2,1)S(1)}, bf16[256,384]{1,0:T(8,128)(2,1)}, u32[]{:S(2)}) copy-start(bf16[256,384]{1,0:T(8,128)(2,1)} %param.11) | copy-start | bytes 589828
  140.6 9.3 %copy-start.2 = (bf16[256,384]{1,0:T(8,128)(2,1)S(1)}, bf16[256,384]{1,0:T(8,128)(2,1)}, u32[]{:S(2)}) copy-start(bf16[256,384]{1,0:T(8,128)(2,1)} %param.12) | copy-start | bytes 589828
  140.6 9.6 %copy-start.5 = (f32[384]{0:T(512)S(1)}, f32[384]{0:T(512)}, u32[]{:S(2)}) copy-start(f32[384]{0:T(512)} %param.14) | copy-start | bytes 4612
  140.6 149.2 %all-to-all-start = ((bf16[384,8,864]{0,2,1:T(8,128)(2,1)}), bf16[384,8,864]{0,2,1:T(8,128)(2,1)}, u32[]{:S(2)}, u32[]{:S(2)}) async-start(bf16[384,8,864]{0,2,1:T(8,128)(2,1)} %copy.19), calls=%async_computation | async-start | bytes 10616832 | tf_op jit(solution)/shard_map/all_to_all | solution.py:79
  145.5 59.8 %copy-start.6 = (bf16[256,384]{1,0:T(8,128)(2,1)S(1)}, bf16[256,384]{1,0:T(8,128)(2,1)}, u32[]{:S(2)}) copy-start(bf16[256,384]{1,0:T(8,128)(2,1)} %param.9) | copy-start | bytes 589828
  145.5 137.8 %all-gather.4.cloned.1.call-start = ((), (), s32[]{:S(2)}) async-start(), calls=%async_computation.1 | async-start | bytes 1769472 | tf_op jit(solution)/shard_map/all_gather | solution.py:77
  145.6 59.6 %collective-permute-start = (bf16[2,128,384]{2,1,0:T(8,128)(2,1)S(1)}, bf16[2,128,384]{2,1,0:T(8,128)(2,1)S(1)}, u32[]{:S(2)}, u32[]{:S(2)}) collective-permute-start(bf16[2,128,384]{2,1,0:T(8,128)(2,1)S(1)} %get-tuple-element.10), channel_id=1, source_target_pairs={{0,8},{8,16},{16,24},{24,32},{32,40},{40,48},{48,56},{56,64},{64,7... | collective-permute-start | bytes 589832 | tf_op jit(solution)/shard_map/ppermute | solution.py:20
  147.8 57.5 %collective-permute-start.1 = (bf16[2,128,384]{2,1,0:T(8,128)(2,1)S(1)}, bf16[2,128,384]{2,1,0:T(8,128)(2,1)S(1)}, u32[]{:S(2)}, u32[]{:S(2)}) collective-permute-start(bf16[2,128,384]{2,1,0:T(8,128)(2,1)S(1)} %get-tuple-element.11), channel_id=1, source_target_pairs={{8,0},{16,8},{24,16},{32,24},{40,32},{48,40},{56,48},{64,56},{72,6... | collective-permute-start | bytes 589832 | tf_op jit(solution)/shard_map/ppermute | solution.py:22
  207.3 0.7 copy-start.3
  207.3 32.5 %copy-start.4 = (f32[384]{0:T(512)S(1)}, f32[384]{0:T(512)}, u32[]{:S(2)}) copy-start(f32[384]{0:T(512)} %param.15) | copy-start | bytes 4612
  289.8 3.5 %copy-start.7 = (f32[864]{0:T(1024)S(1)}, f32[864]{0:T(1024)}, u32[]{:S(2)}) copy-start(f32[864]{0:T(1024)} %param.17) | copy-start | bytes 10372
Sparse Core Ops, SparseCore 0:
  12.1 106.0 all-gather.5
Sparse Core Ops, SparseCore 1:
  240.8 42.5 all-gather.3
where the time goes:
time: 308 us; the launch traced here: 303 us
  waiting for transfers between devices  207 us (67%)
  local copies, waits for them, and re-layouts  33.8 us (11%)
  blocking collectives  31.6 us (10%)
  between operations  15.7 us (5%)
  starting transfers between devices  9.26 us (3%)
  matrix products  4.24 us (1%)
    all_gather x1, waiting for transfers between devices, shards(): strided = lax.all_gather(w_up, 'ctx', axis=0, tiled=True)  110 us
    ppermute x1, waiting for transfers between devices, padded_2(): lax.ppermute(tail, axis, [(i, (i + 1) % count) for i in range(ends)])  55 us
    all_gather x1, waiting for transfers between devices, shards(): full_feat = lax.all_gather(normed, 'fsdp', axis=1, tiled=True)  41.8 us
    all_to_all x3, local copies, waits for them, and re-layouts, shards(): lax.all_to_all(strided, 'fsdp', split_axis=1, concat_axis=0, tiled=True)  25.9 us
    psum x1, blocking collectives, shards(): row_sum = lax.psum(jnp.sum(rows_float, axis=1), 'fsdp')  19 us
    psum x1, blocking collectives, shards(): var_val = lax.psum(jnp.sum(centered * centered, axis=1), 'fsdp') / D  12.6 us
  transfers between devices with their start and end apart: 5, of which 3 were waited for; matrix products, arithmetic and copies ran while one was open for 4% of the time, Pallas kernels for 0%

commit v1 on v0

v1 whole, which is shorter than its diff:
```python
import functools
import math

import jax
import jax.numpy as jnp
from jax import lax
from jax.experimental import pallas as pl
from jax.experimental.pallas import tpu as pltpu
from jax.sharding import PartitionSpec as P

HEAD = 128
NY, NZ, NC = 8, 4, 2

MESH = pl.DeviceIdType.MESH
F32, BF16 = jnp.float32, jnp.bfloat16


def kernel(
    count_f,
    q_hbm,
    k_hbm,
    v_hbm,
    r_hbm,
    gate_hbm,
    scale_hbm,
    shift_hbm,
    w_hbm,
    bias_hbm,
    res_hbm,
    hid_hbm,
    q_buf,
    kv_buf,
    r_buf,
    vec_in,
    w_buf,
    bias_buf,
    w_send,
    w_recv,
    w_pack,
    wall,
    xg,
    xn,
    vecs,
    acc,
    hid_buf,
    local_sem,
    send_sem,
    recv_sem,
):
    tok, feat = q_buf.shape
    reach = tok // 2
    rows = w_buf.shape[0]
    wide = bias_buf.shape[1]
    d_model = feat * count_f
    me = lax.axis_index("ctx")
    f = lax.axis_index("fsdp")
    count_c = NY * NZ * NC
    y = lax.div(me, NZ * NC)
    zh = lax.rem(lax.div(me, NC), NZ)
    core = lax.rem(me, NC)

    def ctx_of(yy, zz, cc):
        return (yy * NZ + zz) * NC + cc

    right = (ctx_of(lax.rem(y + 1, NY), zh, core), f)
    left = (ctx_of(lax.rem(y + NY - 1, NY), zh, core), f)
    sibling = (ctx_of(y, zh, 1 - core), f)
    before = (lax.rem(me + count_c - 1, count_c), f)
    after = (lax.rem(me + 1, count_c), f)
    f_peers = [(me, lax.rem(f + d, count_f)) for d in range(1, count_f)]
    z_peers = [(ctx_of(y, lax.rem(zh + d, NZ), core), f) for d in range(1, NZ)]

    partners = [right, left, sibling, before, after] + f_peers + z_peers
    barrier = pltpu.get_barrier_semaphore()
    for dev in partners:
        pl.semaphore_signal(barrier, inc=1, device_id=dev, device_id_type=MESH)

    used = [0]
    loads = []

    def load(src, dst):
        copy = pltpu.make_async_copy(src, dst, local_sem.at[len(loads)])
        copy.start()
        loads.append(copy)
        return copy

    started = []

    def send(src, dst, dev):
        n = used[0]
        used[0] += 1
        copy = pltpu.make_async_remote_copy(
            src_ref=src,
            dst_ref=dst,
            send_sem=send_sem.at[n],
            recv_sem=recv_sem.at[n],
            device_id=dev,
            device_id_type=MESH,
        )
        copy.start()
        started.append(copy)
        return copy

    load_w = load(w_hbm, w_buf)
    load_vec = [
        load(scale_hbm, vec_in.at[0]),
        load(shift_hbm, vec_in.at[1]),
        load(gate_hbm, vec_in.at[2]),
        load(bias_hbm, bias_buf),
    ]
    load_k = load(k_hbm, kv_buf.at[0, pl.ds(reach, tok)])
    load_v = load(v_hbm, kv_buf.at[1, pl.ds(reach, tok)])
    load_q = load(q_hbm, q_buf)
    load_r = load(r_hbm, r_buf)

    load_w.wait()
    w_rows = w_buf[...].astype(F32)
    for g in range(count_f):
        w_send[g, 0:rows, 0:wide] = w_rows[:, g * wide : (g + 1) * wide]
    for copy in load_vec:
        copy.wait()
    vecs[f, 0:1, :] = 1.0 + vec_in[0]
    vecs[f, 1:2, :] = vec_in[1]

    pl.semaphore_wait(barrier, len(partners))

    cols_in = [send(w_send.at[dev[1]], w_recv.at[f], dev) for dev in f_peers]
    halo_in = []
    for i, src in enumerate((k_hbm, v_hbm)):
        halo_in.append(send(src.at[pl.ds(tok - reach, reach)], kv_buf.at[i, pl.ds(0, reach)], after))
        halo_in.append(
            send(src.at[pl.ds(0, reach)], kv_buf.at[i, pl.ds(reach + tok, reach)], before)
        )
    vecs_in = [send(vecs.at[f], vecs.at[f], dev) for dev in f_peers]

    w_recv[f] = w_send[f]
    for copy in cols_in:
        copy.wait_recv()
    for g in range(count_f):
        w_pack[rows * g : rows * (g + 1), :] = w_recv[g, 0:rows, :]
    wall[y, zh, core] = w_pack[...].astype(BF16)
    z_in = [send(wall.at[y, zh, core], wall.at[y, zh, core], dev) for dev in z_peers]

    first_pos = me * tok
    seq_total = tok * count_c
    scale_qk = 1.0 / math.sqrt(HEAD)

    def attend(block):
        start = block * reach
        shape = (reach, 3 * reach)
        row_id = lax.broadcasted_iota(jnp.int32, shape, 0)
        col_id = lax.broadcasted_iota(jnp.int32, shape, 1)
        key_pos = first_pos + (start - reach) + col_id
        offset = col_id - row_id
        allowed = (
            (offset >= 0) & (offset <= 2 * reach) & (key_pos >= 0) & (key_pos < seq_total)
        )
        for h in range(feat // HEAD):
            cols = slice(h * HEAD, (h + 1) * HEAD)
            qs = q_buf[start : start + reach, cols]
            ks = kv_buf[0, start : start + 3 * reach, cols]
            vs = kv_buf[1, start : start + 3 * reach, cols]
            scores = (
                lax.dot_general(qs, ks, (((1,), (1,)), ((), ())), preferred_element_type=F32)
                * scale_qk
            )
            masked = jnp.where(allowed, scores, -jnp.inf)
            row_max = jnp.max(masked, axis=1, keepdims=True)
            terms = jnp.exp(masked - row_max)
            probs = (terms / jnp.sum(terms, axis=1, keepdims=True)).astype(BF16)
            attended = jnp.dot(probs, vs, preferred_element_type=F32).astype(BF16)
            resid = r_buf[start : start + reach, cols].astype(F32)
            gate = vec_in[2, :, cols]
            xg[f, start : start + reach, cols] = (resid + gate * attended.astype(F32)).astype(BF16)
        part = pl.ds(start, reach)
        return [send(xg.at[f, part], xg.at[f, part], dev) for dev in f_peers]

    for copy in (load_k, load_v, load_q, load_r):
        copy.wait()
    for copy in halo_in:
        copy.wait_recv()
    x_in = [attend(0)]

    for copy in z_in:
        copy.wait_recv()

    half = NZ // 2
    reach_y = NY // 2

    def hop(source, part, dev):
        ref = wall.at[source, pl.ds(part * half, half), core]
        return send(ref, ref, dev)

    def share(source):
        ref = wall.at[source, :, core]
        return send(ref, ref, sibling)

    def at(shift):
        return lax.rem(y + shift + NY, NY)

    ring = {}
    for part in range(2):
        ring["r", part] = hop(y, part, right)
        ring["l", 1 - part] = hop(y, 1 - part, left)
    shared = {0: share(y)}

    x_in.append(attend(1))
    store_res = pltpu.make_async_copy(xg.at[f], res_hbm, local_sem.at[len(loads)])
    store_res.start()

    for copy in vecs_in:
        copy.wait_recv()

    def normalise(block):
        for copy in x_in[block]:
            copy.wait_recv()
        part = slice(block * reach, (block + 1) * reach)
        total = jnp.zeros((reach, feat), F32)
        for g in range(count_f):
            total += xg[g, part, :].astype(F32)
        mean = jnp.sum(total, axis=1, keepdims=True) / d_model
        total = jnp.zeros((reach, feat), F32)
        for g in range(count_f):
            centered = xg[g, part, :].astype(F32) - mean
            total += centered * centered
        inv = lax.rsqrt(jnp.sum(total, axis=1, keepdims=True) / d_model + 1e-06)
        for g in range(count_f):
            centered = xg[g, part, :].astype(F32) - mean
            xn[g, part, :] = (centered * inv * vecs[g, 0:1, :] + vecs[g, 1:2, :]).astype(BF16)

    def multiply(shift, first=False):
        shared[shift].wait_recv()
        source = at(shift)
        weights = wall[source].reshape(NZ * NC * rows * count_f, wall.shape[-1])
        part = jnp.dot(xn[source], weights, preferred_element_type=F32)
        if first:
            acc[...] = part
        else:
            acc[...] += part

    for step in range(1, reach_y):
        for part in range(2):
            for way, dev, sign in (("r", right, -1), ("l", left, 1)):
                piece = part if way == "r" else 1 - part
                ring[way, piece].wait_recv()
                if step + 1 < reach_y or piece == (0 if way == "r" else 1):
                    ring[way, piece] = hop(at(sign * step), piece, dev)
        shared[-step] = share(at(-step))
        shared[step] = share(at(step))
        if step == 1:
            normalise(0)
        elif step == 2:
            normalise(1)
            multiply(0, first=True)
        else:
            multiply(-1)
            multiply(1)
    multiply(-2)
    multiply(2)
    ring["r", 0].wait_recv()
    ring["l", 1].wait_recv()
    shared[reach_y] = share(at(reach_y))
    multiply(-3)
    multiply(3)
    multiply(reach_y)

    pre = acc[:, 0:wide] + bias_buf[...]
    hid_buf[...] = jax.nn.gelu(pre, approximate=True).astype(BF16)
    store_hid = pltpu.make_async_copy(hid_buf, hid_hbm, local_sem.at[len(loads) + 1])
    store_hid.start()
    for copy in started:
        copy.wait_send()
    store_res.wait()
    store_hid.wait()


def shards(query_act, key_act, value_act, resid_in, gate_vec, mod_scale, mod_shift, w_up, bias_up):
    tok, feat = query_act.shape
    count_f = lax.axis_size("fsdp")
    wide = bias_up.shape[0]
    padded = -(-wide // 128) * 128
    rows = w_up.shape[0]
    row_pad = -(-rows // 8) * 8
    sends = 4 * (count_f - 1) + 4 + (NZ - 1) + 2 * (NY - 1) + NY
    anywhere = pl.BlockSpec(memory_space=pl.ANY)
    return pl.pallas_call(
        functools.partial(kernel, count_f),
        out_shape=(
            jax.ShapeDtypeStruct((tok, feat), BF16),
            jax.ShapeDtypeStruct((tok, wide), BF16),
        ),
        in_specs=[anywhere] * 9,
        out_specs=(anywhere, anywhere),
        scratch_shapes=[
            pltpu.VMEM((tok, feat), BF16),
            pltpu.VMEM((2, 2 * tok, feat), BF16),
            pltpu.VMEM((tok, feat), BF16),
            pltpu.VMEM((3, 1, feat), F32),
            pltpu.VMEM((rows, w_up.shape[1]), BF16),
            pltpu.VMEM((1, wide), F32),
            pltpu.VMEM((count_f, row_pad, padded), F32),
            pltpu.VMEM((count_f, row_pad, padded), F32),
            pltpu.VMEM((rows * count_f, padded), F32),
            pltpu.VMEM((NY, NZ, NC, rows * count_f, padded), BF16),
            pltpu.VMEM((count_f, tok, feat), BF16),
            pltpu.VMEM((count_f, tok, feat), BF16),
            pltpu.VMEM((count_f, 8, feat), F32),
            pltpu.VMEM((tok, padded), F32),
            pltpu.VMEM((tok, wide), BF16),
            pltpu.SemaphoreType.DMA((11,)),
            pltpu.SemaphoreType.DMA((sends,)),
            pltpu.SemaphoreType.DMA((sends,)),
        ],
        compiler_params=pltpu.CompilerParams(
            collective_id=0, has_side_effects=True, vmem_limit_bytes=48 * 1024 * 1024
        ),
    )(
        query_act,
        key_act,
        value_act,
        resid_in,
        gate_vec.reshape(1, feat),
        mod_scale.reshape(1, feat),
        mod_shift.reshape(1, feat),
        w_up,
        bias_up.reshape(1, wide),
    )


def solution(mesh):
    placed = (
        P("ctx", "fsdp"),
        P("ctx", "fsdp"),
        P("ctx", "fsdp"),
        P("ctx", "fsdp"),
        P("fsdp"),
        P("fsdp"),
        P("fsdp"),
        P(("ctx", "fsdp"), None),
        P("fsdp"),
    )
    return jax.shard_map(
        shards,
        mesh=mesh,
        in_specs=placed,
        out_specs=(P("ctx", "fsdp"), P("ctx", "fsdp")),
        check_vma=False,
    )
```

time: 308 us -> 70.1 us (0.23); the launches traced: 303 us -> 69.5 us
  waiting for transfers between devices: 207 us -> 0 us
  Pallas kernels: 0 us -> 61.2 us
  blocking collectives: 31.6 us -> 0 us
  local copies, waits for them, and re-layouts: 33.8 us -> 7.62 us
  between operations: 15.7 us -> 0.68 us
  starting transfers between devices: 9.26 us -> 0 us
  matrix products: 4.24 us -> 0 us
    all_gather x2 -> x0, waiting for transfers between devices: 151 us -> none  [the longest x1 110 us: shards(): strided = lax.all_gather(w_up, 'ctx', axis=0, tiled=True)]
    pallas_call x0 -> x1, Pallas kernels: none -> 61.2 us  [shards(): pl.pallas_call(functools.partial(kernel, count_f), out_shape=(jax.ShapeDt...]
    ppermute x2 -> x0, waiting for transfers between devices: 55 us -> none  [the longest x1 55 us: padded_2(): lax.ppermute(tail, axis, [(i, (i + 1) % count) for i in range(ends)])]
    psum x2 -> x0, blocking collectives: 31.6 us -> none  [the longest x1 19 us: shards(): row_sum = lax.psum(jnp.sum(rows_float, axis=1), 'fsdp')]
    all_to_all x3 -> x0, local copies, waits for them, and re-layouts: 25.9 us -> none  [shards(): lax.all_to_all(strided, 'fsdp', split_axis=1, concat_axis=0, tiled=True)]
    all_to_all x1 -> x0, starting transfers between devices: 4.84 us -> none  [shards(): lax.all_to_all(strided, 'fsdp', split_axis=1, concat_axis=0, tiled=True)]
    unnamed x18 -> x17, local copies, waits for them, and re-layouts: 1.4 us -> 5.95 us
    reshape x2 -> x4, local copies, waits for them, and re-layouts: 5.04 us -> 0.7 us  [the longest x1 0.7 us: shards(): gate_vec.reshape(1, feat)]
  transfers between devices with their start and end apart: 5 -> 0, of which waited for: 3 -> 0; matrix products, arithmetic and copies ran while one was open for 4% -> 0% of each run, Pallas kernels for 0% -> 0%
where the time goes in v1:
time: 70.1 us; the launch traced here: 69.5 us
  Pallas kernels  61.2 us (87%)
  local copies, waits for them, and re-layouts  7.62 us (11%)
    pallas_call x1, Pallas kernels, shards(): pl.pallas_call(functools.partial(kernel, count_f), out_shape=(jax.ShapeDt...  61.2 us
    unnamed x17, local copies, waits for them, and re-layouts  5.95 us

profile of v1, /device:TPU:1, one launch (start us, length us, event | category | flops | bytes accessed | tf_op | source)
XLA Modules:
  0.0 69.5 jit_solution(13940877014615423776)
XLA Ops:
  0.6 0.0 copy-start.6
  0.6 0.0 copy-start.7
  0.7 0.7 reshape.16.gate_hbm
  1.3 0.0 copy-done.6
  1.3 0.0 copy-start.5
  1.4 0.0 copy-done.7
  1.4 0.7 copy-done.5
  2.0 0.0 copy-start
  2.0 0.9 %copy-done = bf16[256,384]{1,0:T(8,128)(2,1)S(1)} copy-done((bf16[256,384]{1,0:T(8,128)(2,1)S(1)}, bf16[256,384]{1,0:T(8,128)(2,1)}, u32[]{:S(2)}) %copy-start) | copy-done | bytes 196632
  3.0 0.0 copy-start.1
  3.0 0.9 %copy-done.1 = bf16[256,384]{1,0:T(8,128)(2,1)S(1)} copy-done((bf16[256,384]{1,0:T(8,128)(2,1)S(1)}, bf16[256,384]{1,0:T(8,128)(2,1)}, u32[]{:S(2)}) %copy-start.1) | copy-done | bytes 196632
  3.9 0.0 copy-start.2
  3.9 0.9 %copy-done.2 = bf16[256,384]{1,0:T(8,128)(2,1)S(1)} copy-done((bf16[256,384]{1,0:T(8,128)(2,1)S(1)}, bf16[256,384]{1,0:T(8,128)(2,1)}, u32[]{:S(2)}) %copy-start.2) | copy-done | bytes 196632
  4.8 0.0 copy-start.3
  4.8 0.9 %copy-done.3 = bf16[256,384]{1,0:T(8,128)(2,1)S(1)} copy-done((bf16[256,384]{1,0:T(8,128)(2,1)S(1)}, bf16[256,384]{1,0:T(8,128)(2,1)}, u32[]{:S(2)}) %copy-start.3) | copy-done | bytes 196632
  5.7 0.0 copy-start.4
  5.8 0.9 %copy-done.4 = bf16[6,6912]{1,0:T(8,128)(2,1)S(1)} copy-done((bf16[6,6912]{1,0:T(8,128)(2,1)S(1)}, bf16[6,6912]{1,0:T(8,128)(2,1)}, u32[]{:S(2)}) %copy-start.4) | copy-done | bytes 82968
  6.6 61.2 %shard_map.104 = (bf16[256,384]{1,0:T(8,128)(2,1)S(1)}, bf16[256,864]{1,0:T(8,128)(2,1)S(1)}) custom-call(bf16[256,384]{1,0:T(8,128)(2,1)S(1)} %copy-done, bf16[256,384]{1,0:T(8,128)(2,1)S(1)} %copy-done.1, bf16[256,384]{1,0:T(8,128)(2,1)S(1)} %copy-done.2, bf16[256,384]{1,0:T(8,128)(2,1)S(1)} %copy-done.3, f32[1,384]{1,0:T(1,128)S(1)} %reshape.16.gate_hbm, ...), custom_call_target="tpu_custom_call" | custom-call | tf_op jit(solution)/shard_map/pallas_call | solution.py:286
  67.9 1.0 %copy.11 = bf16[256,864]{0,1:T(8,128)(2,1)} copy(bf16[256,864]{1,0:T(8,128)(2,1)S(1)} %get-tuple-element.3) | data formatting | bytes 884736 | tf_op jit(solution)/shard_map/pallas_call | solution.py:286
  68.9 0.7 copy.13
  (3 shorter events, 0.0 us)
Async XLA Ops:
  0.6 0.7 %copy-start.6 = (f32[384]{0:T(512)S(1)}, f32[384]{0:T(512)}, u32[]{:S(2)}) copy-start(f32[384]{0:T(512)} %param.14) | copy-start | bytes 4612
  0.6 0.7 %copy-start.7 = (f32[384]{0:T(512)S(1)}, f32[384]{0:T(512)}, u32[]{:S(2)}) copy-start(f32[384]{0:T(512)} %param.15) | copy-start | bytes 4612
  1.3 0.7 copy-start.5
  2.0 0.9 %copy-start = (bf16[256,384]{1,0:T(8,128)(2,1)S(1)}, bf16[256,384]{1,0:T(8,128)(2,1)}, u32[]{:S(2)}) copy-start(bf16[256,384]{1,0:T(8,128)(2,1)} %q_hbm.1) | copy-start | bytes 589828
  3.0 0.9 %copy-start.1 = (bf16[256,384]{1,0:T(8,128)(2,1)S(1)}, bf16[256,384]{1,0:T(8,128)(2,1)}, u32[]{:S(2)}) copy-start(bf16[256,384]{1,0:T(8,128)(2,1)} %k_hbm.1) | copy-start | bytes 589828
  3.9 0.9 %copy-start.2 = (bf16[256,384]{1,0:T(8,128)(2,1)S(1)}, bf16[256,384]{1,0:T(8,128)(2,1)}, u32[]{:S(2)}) copy-start(bf16[256,384]{1,0:T(8,128)(2,1)} %v_hbm.1) | copy-start | bytes 589828
  4.8 0.9 %copy-start.3 = (bf16[256,384]{1,0:T(8,128)(2,1)S(1)}, bf16[256,384]{1,0:T(8,128)(2,1)}, u32[]{:S(2)}) copy-start(bf16[256,384]{1,0:T(8,128)(2,1)} %r_hbm.1) | copy-start | bytes 589828
  5.7 0.9 %copy-start.4 = (bf16[6,6912]{1,0:T(8,128)(2,1)S(1)}, bf16[6,6912]{1,0:T(8,128)(2,1)}, u32[]{:S(2)}) copy-start(bf16[6,6912]{1,0:T(8,128)(2,1)} %w_hbm.1) | copy-start | bytes 248836

commit v2 on v1

v2 whole, which is shorter than its diff:
```python
import functools
import math

import jax
import jax.numpy as jnp
from jax import lax
from jax.experimental import pallas as pl
from jax.experimental.pallas import tpu as pltpu
from jax.sharding import PartitionSpec as P

HEAD = 128
NY, NZ, NC = 8, 4, 2
NX = 4

MESH = pl.DeviceIdType.MESH
F32, BF16 = jnp.float32, jnp.bfloat16


def kernel(
    count_f,
    q_hbm,
    k_hbm,
    v_hbm,
    r_hbm,
    gate_hbm,
    scale_hbm,
    shift_hbm,
    w_hbm,
    bias_hbm,
    res_hbm,
    hid_hbm,
    q_buf,
    kv_buf,
    r_buf,
    scale_buf,
    shift_buf,
    gate_buf,
    w_buf,
    bias_buf,
    w_send,
    w_recv,
    w_pack,
    wall,
    xg,
    xn,
    vecs,
    acc,
    hid_buf,
    local_sem,
    send_sem,
    recv_sem,
    ready_sem,
):
    tok, feat = q_buf.shape
    reach = tok // 2
    rows = w_buf.shape[0]
    wide = bias_buf.shape[0]
    d_model = feat * count_f
    me = lax.axis_index("ctx")
    f = lax.axis_index("fsdp")
    count_c = NY * NZ * NC
    y = lax.div(me, NZ * NC)
    zh = lax.rem(lax.div(me, NC), NZ)
    core = lax.rem(me, NC)
    odd = lax.rem(zh, 2)
    zs = (zh, zh + 1 - 2 * odd, lax.rem(zh + 2, NZ), NZ - 1 - zh)
    late = lax.div(zh, 2)

    def ctx_of(yy, zz, cc):
        return (yy * NZ + zz) * NC + cc

    right = (ctx_of(lax.rem(y + 1, NY), zh, core), f)
    left = (ctx_of(lax.rem(y + NY - 1, NY), zh, core), f)
    sibling = (ctx_of(y, zh, 1 - core), f)
    f_peers = [(me, lax.rem(f + d, count_f)) for d in range(1, count_f)]
    row = lax.div(f, NX) * NX
    x_peers = [(me, row + lax.rem(f + d, NX)) for d in (1, 3, 2)]
    beside = lax.rem(f + NX, count_f)
    z_peers = [None] + [(ctx_of(y, zs[j], core), f) for j in range(1, NZ)]
    far = (lax.rem(me + 2 * core - 1 + count_c, count_c), f)
    crossing = 1 - lax.rem(odd + core, 2)

    barrier = pltpu.get_barrier_semaphore()
    near = [right, left, sibling, z_peers[1]] + f_peers

    def greet(dev):
        pl.semaphore_signal(barrier, inc=1, device_id=dev, device_id_type=MESH)

    for dev in near:
        greet(dev)

    @pl.when(late == 0)
    def _():
        greet(z_peers[3])

    @pl.when(late * crossing == 0)
    def _():
        greet(far)

    used = [0]
    loads = []

    def load(src, dst):
        copy = pltpu.make_async_copy(src, dst, local_sem.at[len(loads)])
        copy.start()
        loads.append(copy)
        return copy

    started = []

    def prepare(src, dst, dev):
        n = used[0]
        used[0] += 1
        copy = pltpu.make_async_remote_copy(
            src_ref=src,
            dst_ref=dst,
            send_sem=send_sem.at[n],
            recv_sem=recv_sem.at[n],
            device_id=dev,
            device_id_type=MESH,
        )
        started.append(copy)
        return copy

    def send(src, dst, dev):
        copy = prepare(src, dst, dev)
        copy.start()
        return copy

    load_w = load(w_hbm, w_buf)
    load_k = load(k_hbm, kv_buf.at[0, pl.ds(reach, tok)])
    load_v = load(v_hbm, kv_buf.at[1, pl.ds(reach, tok)])
    load_q = load(q_hbm, q_buf)
    load_r = load(r_hbm, r_buf)
    load_vec = [
        load(scale_hbm, scale_buf),
        load(shift_hbm, shift_buf),
        load(gate_hbm, gate_buf),
        load(bias_hbm, bias_buf),
    ]

    load_w.wait()
    w_rows = w_buf[...].astype(F32)
    for g in range(count_f):
        w_send[g, 0:rows, 0:wide] = w_rows[:, g * wide : (g + 1) * wide].astype(BF16)
    for copy in [load_k, load_v, load_q, load_r] + load_vec:
        copy.wait()
    vecs[f, 0:1, :] = 1.0 + scale_buf[...].reshape(1, feat)
    vecs[f, 1:2, :] = shift_buf[...].reshape(1, feat)

    pl.semaphore_wait(barrier, len(near) + (1 - crossing) + late * (1 + crossing))

    cols_in = [send(w_send.at[dev[1]], w_recv.at[f], dev) for dev in f_peers]
    own_edge = pl.multiple_of(reach + (1 - core) * reach, reach)
    far_edge = pl.multiple_of(reach + core * reach, reach)
    low_halo, high_halo = 0, reach + tok
    near_slot = pl.multiple_of((1 - core) * low_halo + core * high_halo, reach)
    far_slot = pl.multiple_of((1 - core) * high_halo + core * low_halo, reach)
    near_halo = send(kv_buf.at[:, pl.ds(own_edge, reach)], kv_buf.at[:, pl.ds(near_slot, reach)], sibling)
    far_halo = prepare(kv_buf.at[:, pl.ds(far_edge, reach)], kv_buf.at[:, pl.ds(far_slot, reach)], far)

    @pl.when(late == 1)
    def _():
        pl.semaphore_signal(ready_sem.at[0], inc=1, device_id=z_peers[3], device_id_type=MESH)

    @pl.when(late * crossing == 1)
    def _():
        pl.semaphore_signal(ready_sem.at[1], inc=1, device_id=far, device_id_type=MESH)

    asks = (1 - late) * crossing

    @pl.when(asks == 0)
    def _():
        far_halo.start()

    w_recv[f] = w_send[f]
    for copy in cols_in:
        copy.wait_recv()
    for g in range(count_f):
        w_pack[rows * g : rows * (g + 1), :] = w_recv[g, 0:rows, :].astype(F32)
    wall[y, zh, core] = w_pack[...].astype(BF16)
    mine = wall.at[y, zh, core]

    ring = {}
    reach_y = NY // 2
    hops = {0: (reach_y, reach_y - 1), 1: (reach_y - 1, reach_y)}

    def at(shift):
        return lax.rem(y + shift + NY, NY)

    def pass_on(j, hop):
        for way, dev, sign in ((0, right, -1), (1, left, 1)):
            last = hops[j % 2][way]
            if 1 <= hop <= last:
                ring[j, way].wait_recv()
            if hop < last:
                ref = wall.at[at(sign * hop), zs[j], core]
                ring[j, way] = send(ref, ref, dev)

    def half_of(j):
        return lax.div(zs[j], 2)

    shared = {}

    def share(j, shift):
        ref = wall.at[at(shift), pl.ds(2 * half_of(j), 2), core]
        shared[j, shift] = send(ref, ref, sibling)

    pass_on(0, 0)
    z_in = [None, send(mine, mine, z_peers[1])]
    z_in += [None, prepare(mine, mine, z_peers[3])]

    @pl.when(late == 1)
    def _():
        z_in[3].start()

    vecs_in = [send(vecs.at[f], vecs.at[f], dev) for dev in f_peers]

    first_pos = me * tok
    seq_total = tok * count_c
    scale_qk = 1.0 / math.sqrt(HEAD)

    def attend(block):
        start = pl.multiple_of(block * reach, reach)
        part = pl.ds(start, reach)
        shape = (reach, 3 * reach)
        row_id = lax.broadcasted_iota(jnp.int32, shape, 0)
        col_id = lax.broadcasted_iota(jnp.int32, shape, 1)
        key_pos = first_pos + (start - reach) + col_id
        offset = col_id - row_id
        allowed = (
            (offset >= 0) & (offset <= 2 * reach) & (key_pos >= 0) & (key_pos < seq_total)
        )
        for h in range(feat // HEAD):
            cols = slice(h * HEAD, (h + 1) * HEAD)
            qs = q_buf[part, cols]
            ks = kv_buf[0, pl.ds(start, 3 * reach), cols]
            vs = kv_buf[1, pl.ds(start, 3 * reach), cols]
            scores = (
                lax.dot_general(qs, ks, (((1,), (1,)), ((), ())), preferred_element_type=F32)
                * scale_qk
            )
            masked = jnp.where(allowed, scores, -jnp.inf)
            row_max = jnp.max(masked, axis=1, keepdims=True)
            terms = jnp.exp(masked - row_max)
            probs = (terms / jnp.sum(terms, axis=1, keepdims=True)).astype(BF16)
            attended = jnp.dot(probs, vs, preferred_element_type=F32).astype(BF16)
            resid = r_buf[part, cols].astype(F32)
            gate = gate_buf[cols].reshape(1, HEAD)
            xg[f, part, cols] = (resid + gate * attended.astype(F32)).astype(BF16)
        mine = xg.at[f, part]
        return [send(mine, mine, dev) for dev in [(me, beside)] + x_peers]

    def part_of(order):
        return pl.ds(pl.multiple_of(((1 - core) if order == 0 else core) * reach, reach), reach)

    def relay(order):
        x_in[order].pop(0).wait_recv()
        theirs = xg.at[beside, part_of(order)]
        x_in[order] += [send(theirs, theirs, dev) for dev in x_peers]

    def normalise(order):
        for copy in x_in[order]:
            copy.wait_recv()
        part = part_of(order)
        total = jnp.zeros((reach, feat), F32)
        for g in range(count_f):
            total += xg[g, part, :].astype(F32)
        mean = jnp.sum(total, axis=1, keepdims=True) / d_model
        total = jnp.zeros((reach, feat), F32)
        for g in range(count_f):
            centered = xg[g, part, :].astype(F32) - mean
            total += centered * centered
        inv = lax.rsqrt(jnp.sum(total, axis=1, keepdims=True) / d_model + 1e-06)
        for g in range(count_f):
            centered = xg[g, part, :].astype(F32) - mean
            xn[g, part, :] = (centered * inv * vecs[g, 0:1, :] + vecs[g, 1:2, :]).astype(BF16)

    def multiply(shift, first=False):
        shared[1, shift].wait_recv()
        shared[3, shift].wait_recv()
        source = at(shift)
        weights = wall[source].reshape(NZ * NC * rows * count_f, wall.shape[-1])
        part = jnp.dot(xn[source], weights, preferred_element_type=F32)
        if first:
            acc[...] = part
        else:
            acc[...] += part

    near_halo.wait_recv()
    x_in = [attend(1 - core)]
    pass_on(0, 1)

    @pl.when(late == 0)
    def _():
        pl.semaphore_wait(ready_sem.at[0], 1)
        z_in[3].start()

    @pl.when(asks == 1)
    def _():
        pl.semaphore_wait(ready_sem.at[1], 1)
        far_halo.start()

    z_in[1].wait_recv()
    pass_on(1, 0)
    relay(0)
    share(1, 0)
    pass_on(0, 2)
    pass_on(1, 1)
    far_halo.wait_recv()
    x_in.append(attend(core))
    store_res = pltpu.make_async_copy(xg.at[f], res_hbm, local_sem.at[len(loads)])
    store_res.start()
    pass_on(0, 3)
    share(1, -1)
    share(1, 1)
    z_in[3].wait_recv()
    theirs = wall.at[y, zs[3], core]
    z_in[2] = send(theirs, theirs, z_peers[1])
    pass_on(3, 0)
    pass_on(1, 2)
    share(1, -2)
    share(1, 2)
    relay(1)
    z_in[2].wait_recv()
    pass_on(2, 0)
    share(3, 0)
    pass_on(0, 4)
    pass_on(1, 3)
    share(1, -3)
    share(1, 3)
    pass_on(3, 1)
    for copy in vecs_in:
        copy.wait_recv()
    normalise(0)
    pass_on(2, 1)
    share(3, -1)
    share(3, 1)
    pass_on(1, 4)
    share(1, reach_y)
    pass_on(3, 2)
    pass_on(2, 2)
    share(3, -2)
    share(3, 2)
    normalise(1)
    multiply(0, first=True)
    pass_on(3, 3)
    pass_on(2, 3)
    share(3, -3)
    share(3, 3)
    multiply(-1)
    multiply(1)
    multiply(-2)
    multiply(2)
    pass_on(3, 4)
    pass_on(2, 4)
    share(3, reach_y)
    multiply(-3)
    multiply(3)
    multiply(reach_y)

    pre = acc[:, 0:wide] + bias_buf[...].reshape(1, wide)
    hid_buf[...] = jax.nn.gelu(pre, approximate=True).astype(BF16)
    store_hid = pltpu.make_async_copy(hid_buf, hid_hbm, local_sem.at[len(loads) + 1])
    store_hid.start()
    for copy in started:
        copy.wait_send()
    store_res.wait()
    store_hid.wait()


def shards(query_act, key_act, value_act, resid_in, gate_vec, mod_scale, mod_shift, w_up, bias_up):
    tok, feat = query_act.shape
    count_f = lax.axis_size("fsdp")
    wide = bias_up.shape[0]
    padded = -(-wide // 128) * 128
    rows = w_up.shape[0]
    row_pad = -(-rows // 8) * 8
    sends = 4 * (count_f - 1) + 2 + (NZ - 1) + NZ * (NY - 1) + 2 * NY
    anywhere = pl.BlockSpec(memory_space=pl.ANY)
    return pl.pallas_call(
        functools.partial(kernel, count_f),
        out_shape=(
            jax.ShapeDtypeStruct((tok, feat), BF16),
            jax.ShapeDtypeStruct((tok, wide), BF16),
        ),
        in_specs=[anywhere] * 9,
        out_specs=(anywhere, anywhere),
        scratch_shapes=[
            pltpu.VMEM((tok, feat), BF16),
            pltpu.VMEM((2, 2 * tok, feat), BF16),
            pltpu.VMEM((tok, feat), BF16),
            pltpu.VMEM((feat,), F32),
            pltpu.VMEM((feat,), F32),
            pltpu.VMEM((feat,), F32),
            pltpu.VMEM((rows, w_up.shape[1]), BF16),
            pltpu.VMEM((wide,), F32),
            pltpu.VMEM((count_f, row_pad, padded), BF16),
            pltpu.VMEM((count_f, row_pad, padded), BF16),
            pltpu.VMEM((rows * count_f, padded), F32),
            pltpu.VMEM((NY, NZ, NC, rows * count_f, padded), BF16),
            pltpu.VMEM((count_f, tok, feat), BF16),
            pltpu.VMEM((count_f, tok, feat), BF16),
            pltpu.VMEM((count_f, 2, feat), F32),
            pltpu.VMEM((tok, padded), F32),
            pltpu.VMEM((tok, wide), BF16),
            pltpu.SemaphoreType.DMA((11,)),
            pltpu.SemaphoreType.DMA((sends,)),
            pltpu.SemaphoreType.DMA((sends,)),
            pltpu.SemaphoreType.REGULAR((2,)),
        ],
        compiler_params=pltpu.CompilerParams(
            collective_id=0, has_side_effects=True, vmem_limit_bytes=60 * 1024 * 1024
        ),
    )(
        query_act,
        key_act,
        value_act,
        resid_in,
        gate_vec,
        mod_scale,
        mod_shift,
        w_up,
        bias_up,
    )


def solution(mesh):
    placed = (
        P("ctx", "fsdp"),
        P("ctx", "fsdp"),
        P("ctx", "fsdp"),
        P("ctx", "fsdp"),
        P("fsdp"),
        P("fsdp"),
        P("fsdp"),
        P(("ctx", "fsdp"), None),
        P("fsdp"),
    )
    return jax.shard_map(
        shards,
        mesh=mesh,
        in_specs=placed,
        out_specs=(P("ctx", "fsdp"), P("ctx", "fsdp")),
        check_vma=False,
    )
```

time: 70.1 us -> 59.1 us (0.84)
  Pallas kernels: 61.2 us -> 55.6 us
  local copies, waits for them, and re-layouts: 7.62 us -> 2.7 us
    pallas_call x1, Pallas kernels: 61.2 us -> 55.6 us  [shards(): pl.pallas_call(functools.partial(kernel, count_f), out_shape=(jax.ShapeDt...]
    unnamed x17 -> x3, local copies, waits for them, and re-layouts: 5.95 us -> 0.68 us
    pallas_call x1, local copies, waits for them, and re-layouts: 0.97 us -> 2.02 us  [shards(): pl.pallas_call(functools.partial(kernel, count_f), out_shape=(jax.ShapeDt...]
    reshape x4 -> x0, local copies, waits for them, and re-layouts: 0.7 us -> none  [the longest x1 0.7 us: shards(): gate_vec.reshape(1, feat)]
where the time goes in v2:
time: 59.1 us; the launch traced here: 59 us
  Pallas kernels  55.6 us (94%)
  local copies, waits for them, and re-layouts  2.7 us (5%)
  between operations  0.65 us (1%)
    pallas_call x1, Pallas kernels, shards(): pl.pallas_call(functools.partial(kernel, count_f), out_shape=(jax.ShapeDt...  55.6 us
    pallas_call x1, local copies, waits for them, and re-layouts, shards(): pl.pallas_call(functools.partial(kernel, count_f), out_shape=(jax.ShapeDt...  2.02 us

profile of v2, /device:TPU:1, one launch (start us, length us, event | category | flops | bytes accessed | tf_op | source)
XLA Modules:
  0.0 59.0 jit_solution(17192051391167436129)
XLA Ops:
  0.6 55.6 %shard_map.104 = (bf16[256,384]{1,0:T(8,128)(2,1)}, bf16[256,864]{1,0:T(8,128)(2,1)}) custom-call(bf16[256,384]{1,0:T(8,128)(2,1)} %q_hbm.1, bf16[256,384]{1,0:T(8,128)(2,1)} %k_hbm.1, bf16[256,384]{1,0:T(8,128)(2,1)} %v_hbm.1, bf16[256,384]{1,0:T(8,128)(2,1)} %r_hbm.1, f32[384]{0:T(512)} %gate_hbm.1, f32[384]{0:T(512)} %scale_hbm.1, f32[384]{0:T(512)} %shift_hbm.1, ...), custom_call_target="tpu_custom_call" | custom-call | tf_op jit(solution)/shard_map/pallas_call | solution.py:381
  56.2 0.0 copy-start
  56.3 2.0 %copy.11 = bf16[256,864]{0,1:T(8,128)(2,1)} copy(bf16[256,864]{1,0:T(8,128)(2,1)} %get-tuple-element.3) | data formatting | bytes 884736 | tf_op jit(solution)/shard_map/pallas_call | solution.py:381
  58.3 0.0 copy-done
  58.3 0.7 %copy.13 = bf16[256,384]{1,0:T(8,128)(2,1)} copy(bf16[256,384]{1,0:T(8,128)(2,1)S(1)} %copy-done) | data formatting | bytes 393216
Async XLA Ops:
  56.2 2.0 %copy-start = (bf16[256,384]{1,0:T(8,128)(2,1)S(1)}, bf16[256,384]{1,0:T(8,128)(2,1)}, u32[]{:S(2)}) copy-start(bf16[256,384]{1,0:T(8,128)(2,1)} %get-tuple-element.6) | copy-start | bytes 589828

commit v3 on v2

--- a/solution.py
+++ b/solution.py
@@ -169,33 +169,38 @@
 
     asks = (1 - late) * crossing
 
-    @pl.when(asks == 0)
-    def _():
-        far_halo.start()
-
     w_recv[f] = w_send[f]
     for copy in cols_in:
         copy.wait_recv()
     for g in range(count_f):
         w_pack[rows * g : rows * (g + 1), :] = w_recv[g, 0:rows, :].astype(F32)
     wall[y, zh, core] = w_pack[...].astype(BF16)
-    mine = wall.at[y, zh, core]
 
     ring = {}
     reach_y = NY // 2
-    hops = {0: (reach_y, reach_y - 1), 1: (reach_y - 1, reach_y)}
+    hops = ((reach_y, reach_y - 1), (reach_y - 1, reach_y))
+    tiles = wall.shape[-1] // 128
+    cut = (tiles + 1) // 2 * 128
+    lanes = (pl.ds(0, cut), pl.ds(cut, tiles * 128 - cut))
 
     def at(shift):
         return lax.rem(y + shift + NY, NY)
 
-    def pass_on(j, hop):
+    def piece(source, j, p):
+        return wall.at[source, zs[j], core, :, lanes[p]]
+
+    def pass_on(j, hop, p=None):
+        if p is None:
+            for p in range(len(hops)):
+                pass_on(j, hop, p)
+            return
         for way, dev, sign in ((0, right, -1), (1, left, 1)):
-            last = hops[j % 2][way]
+            last = hops[p][way]
             if 1 <= hop <= last:
-                ring[j, way].wait_recv()
+                ring[j, p, way].wait_recv()
             if hop < last:
-                ref = wall.at[at(sign * hop), zs[j], core]
-                ring[j, way] = send(ref, ref, dev)
+                ref = piece(at(sign * hop), j, p)
+                ring[j, p, way] = send(ref, ref, dev)
 
     def half_of(j):
         return lax.div(zs[j], 2)
@@ -207,14 +212,17 @@
         shared[j, shift] = send(ref, ref, sibling)
 
     pass_on(0, 0)
-    z_in = [None, send(mine, mine, z_peers[1])]
-    z_in += [None, prepare(mine, mine, z_peers[3])]
+    z_in = {}
+    for p in range(len(hops)):
+        z_in[1, p] = send(piece(y, 0, p), piece(y, 0, p), z_peers[1])
+    for p in range(len(hops)):
+        z_in[3, p] = prepare(piece(y, 0, p), piece(y, 0, p), z_peers[3])
 
     @pl.when(late == 1)
     def _():
-        z_in[3].start()
-
-    vecs_in = [send(vecs.at[f], vecs.at[f], dev) for dev in f_peers]
+        for p in range(len(hops)):
+            z_in[3, p].start()
+
 
     first_pos = me * tok
     seq_total = tok * count_c
@@ -291,72 +299,80 @@
     x_in = [attend(1 - core)]
     pass_on(0, 1)
 
+    @pl.when(asks == 0)
+    def _():
+        far_halo.start()
+
     @pl.when(late == 0)
     def _():
         pl.semaphore_wait(ready_sem.at[0], 1)
-        z_in[3].start()
+        for p in range(len(hops)):
+            z_in[3, p].start()
 
     @pl.when(asks == 1)
     def _():
         pl.semaphore_wait(ready_sem.at[1], 1)
         far_halo.start()
 
-    z_in[1].wait_recv()
-    pass_on(1, 0)
+    for p in range(len(hops)):
+        z_in[1, p].wait_recv()
+        pass_on(1, 0, p)
+    pass_on(0, 2)
     relay(0)
+    vecs_in = [send(vecs.at[f], vecs.at[f], dev) for dev in f_peers]
     share(1, 0)
-    pass_on(0, 2)
     pass_on(1, 1)
+    for p in range(len(hops)):
+        z_in[3, p].wait_recv()
+        z_in[2, p] = send(piece(y, 3, p), piece(y, 3, p), z_peers[1])
+        pass_on(3, 0, p)
+    pass_on(0, 3)
     far_halo.wait_recv()
     x_in.append(attend(core))
     store_res = pltpu.make_async_copy(xg.at[f], res_hbm, local_sem.at[len(loads)])
     store_res.start()
-    pass_on(0, 3)
     share(1, -1)
     share(1, 1)
-    z_in[3].wait_recv()
-    theirs = wall.at[y, zs[3], core]
-    z_in[2] = send(theirs, theirs, z_peers[1])
-    pass_on(3, 0)
     pass_on(1, 2)
     share(1, -2)
     share(1, 2)
-    relay(1)
-    z_in[2].wait_recv()
-    pass_on(2, 0)
+    for p in range(len(hops)):
+        z_in[2, p].wait_recv()
+        pass_on(2, 0, p)
     share(3, 0)
     pass_on(0, 4)
+    pass_on(3, 1)
+    relay(1)
     pass_on(1, 3)
     share(1, -3)
     share(1, 3)
-    pass_on(3, 1)
-    for copy in vecs_in:
-        copy.wait_recv()
-    normalise(0)
     pass_on(2, 1)
     share(3, -1)
     share(3, 1)
     pass_on(1, 4)
     share(1, reach_y)
     pass_on(3, 2)
+    for copy in vecs_in:
+        copy.wait_recv()
+    normalise(0)
     pass_on(2, 2)
     share(3, -2)
     share(3, 2)
-    normalise(1)
-    multiply(0, first=True)
     pass_on(3, 3)
     pass_on(2, 3)
     share(3, -3)
     share(3, 3)
+    normalise(1)
+    multiply(0, first=True)
     multiply(-1)
     multiply(1)
     multiply(-2)
     multiply(2)
+    multiply(-3)
+    multiply(3)
     pass_on(3, 4)
     pass_on(2, 4)
     share(3, reach_y)
-    multiply(-3)
-    multiply(3)
     multiply(reach_y)
 
     pre = acc[:, 0:wide] + bias_buf[...].reshape(1, wide)
@@ -376,7 +392,7 @@
     padded = -(-wide // 128) * 128
     rows = w_up.shape[0]
     row_pad = -(-rows // 8) * 8
-    sends = 4 * (count_f - 1) + 2 + (NZ - 1) + NZ * (NY - 1) + 2 * NY
+    sends = 4 * (count_f - 1) + 2 + 2 * (NZ - 1) + 2 * NZ * (NY - 1) + 2 * NY
     anywhere = pl.BlockSpec(memory_space=pl.ANY)
     return pl.pallas_call(
         functools.partial(kernel, count_f),
@@ -410,18 +426,18 @@
             pltpu.SemaphoreType.REGULAR((2,)),
         ],
         compiler_params=pltpu.CompilerParams(
-            collective_id=0, has_side_effects=True, vmem_limit_bytes=60 * 1024 * 1024
+            collective_id=0, has_side_effects=True, vmem_limit_bytes=48 * 1024 * 1024
         ),
     )(
-        query_act,
-        key_act,
-        value_act,
-        resid_in,
-        gate_vec,
-        mod_scale,
-        mod_shift,
-        w_up,
-        bias_up,
+        pltpu.with_memory_space_constraint(query_act, pltpu.HBM),
+        pltpu.with_memory_space_constraint(key_act, pltpu.HBM),
+        pltpu.with_memory_space_constraint(value_act, pltpu.HBM),
+        pltpu.with_memory_space_constraint(resid_in, pltpu.HBM),
+        pltpu.with_memory_space_constraint(gate_vec, pltpu.HBM),
+        pltpu.with_memory_space_constraint(mod_scale, pltpu.HBM),
+        pltpu.with_memory_space_constraint(mod_shift, pltpu.HBM),
+        pltpu.with_memory_space_constraint(w_up, pltpu.HBM),
+        pltpu.with_memory_space_constraint(bias_up, pltpu.HBM),
     )
 
 

time: 59.1 us -> 56.5 us (0.956)
  Pallas kernels: 55.6 us -> 54.1 us
  local copies, waits for them, and re-layouts: 2.7 us -> 1.65 us
    pallas_call x1, Pallas kernels: 55.6 us -> 54.1 us  [shards(): pl.pallas_call(functools.partial(kernel, count_f), out_shape=(jax.ShapeDt...]
    pallas_call x1, local copies, waits for them, and re-layouts: 2.02 us -> 0.97 us  [shards(): pl.pallas_call(functools.partial(kernel, count_f), out_shape=(jax.ShapeDt...]
where the time goes in v3:
time: 56.5 us; the launch traced here: 56.4 us
  Pallas kernels  54.1 us (96%)
  local copies, waits for them, and re-layouts  1.65 us (3%)
  between operations  0.64 us (1%)
    pallas_call x1, Pallas kernels, shards(): pl.pallas_call(functools.partial(kernel, count_f), out_shape=(jax.ShapeDt...  54.1 us

profile of v3, /device:TPU:1, one launch (start us, length us, event | category | flops | bytes accessed | tf_op | source)
XLA Modules:
  0.0 56.4 jit_solution(8192056056971879421)
XLA Ops:
  0.6 54.1 %shard_map.104 = (bf16[256,384]{1,0:T(8,128)(2,1)S(1)}, bf16[256,864]{1,0:T(8,128)(2,1)S(1)}) custom-call(bf16[256,384]{1,0:T(8,128)(2,1)} %q_hbm.1, bf16[256,384]{1,0:T(8,128)(2,1)} %k_hbm.1, bf16[256,384]{1,0:T(8,128)(2,1)} %v_hbm.1, bf16[256,384]{1,0:T(8,128)(2,1)} %r_hbm.1, f32[384]{0:T(512)} %gate_hbm.1, f32[384]{0:T(512)} %scale_hbm.1, f32[384]{0:T(512)} %shift_hbm.1, ...), custom_call_target="tpu_custom_call" | custom-call | tf_op jit(solution)/shard_map/pallas_call | solution.py:397
  54.7 1.0 %copy.11 = bf16[256,864]{0,1:T(8,128)(2,1)} copy(bf16[256,864]{1,0:T(8,128)(2,1)S(1)} %get-tuple-element.3) | data formatting | bytes 884736 | tf_op jit(solution)/shard_map/pallas_call | solution.py:397
  55.7 0.7 %copy.13 = bf16[256,384]{1,0:T(8,128)(2,1)} copy(bf16[256,384]{1,0:T(8,128)(2,1)S(1)} %get-tuple-element.6) | data formatting | bytes 393216

commit v4 on v3

--- a/solution.py
+++ b/solution.py
@@ -295,13 +295,13 @@
         else:
             acc[...] += part
 
+    @pl.when(asks == 0)
+    def _():
+        far_halo.start()
+
     near_halo.wait_recv()
     x_in = [attend(1 - core)]
     pass_on(0, 1)
-
-    @pl.when(asks == 0)
-    def _():
-        far_halo.start()
 
     @pl.when(late == 0)
     def _():

time: 56.5 us -> 56 us (level)
  no operation moved by 1% of the time
where the time goes in v4:
time: 56 us; the launch traced here: 55.9 us
  Pallas kernels  53.6 us (96%)
  local copies, waits for them, and re-layouts  1.65 us (3%)
  between operations  0.64 us (1%)
    pallas_call x1, Pallas kernels, shards(): pl.pallas_call(functools.partial(kernel, count_f), out_shape=(jax.ShapeDt...  53.6 us

profile of v4, /device:TPU:1, one launch (start us, length us, event | category | flops | bytes accessed | tf_op | source)
XLA Modules:
  0.0 55.9 jit_solution(14639311471745159746)
XLA Ops:
  0.6 53.6 %shard_map.104 = (bf16[256,384]{1,0:T(8,128)(2,1)S(1)}, bf16[256,864]{1,0:T(8,128)(2,1)S(1)}) custom-call(bf16[256,384]{1,0:T(8,128)(2,1)} %q_hbm.1, bf16[256,384]{1,0:T(8,128)(2,1)} %k_hbm.1, bf16[256,384]{1,0:T(8,128)(2,1)} %v_hbm.1, bf16[256,384]{1,0:T(8,128)(2,1)} %r_hbm.1, f32[384]{0:T(512)} %gate_hbm.1, f32[384]{0:T(512)} %scale_hbm.1, f32[384]{0:T(512)} %shift_hbm.1, ...), custom_call_target="tpu_custom_call" | custom-call | tf_op jit(solution)/shard_map/pallas_call | solution.py:397
  54.3 1.0 %copy.11 = bf16[256,864]{0,1:T(8,128)(2,1)} copy(bf16[256,864]{1,0:T(8,128)(2,1)S(1)} %get-tuple-element.3) | data formatting | bytes 884736 | tf_op jit(solution)/shard_map/pallas_call | solution.py:397
  55.2 0.7 %copy.13 = bf16[256,384]{1,0:T(8,128)(2,1)} copy(bf16[256,384]{1,0:T(8,128)(2,1)S(1)} %get-tuple-element.6) | data formatting | bytes 393216
